TPU v7x, 128 devices: a whole 4x4x4 slice. The times are simulated.
128 devices in a mesh: tm: 32 (over z, x, core), space: 4 (over y).
Axes of the slice: x: 4, y: 4, z: 4, core: 2. Of those that a mesh axis runs over, the one named last changes fastest.
Arguments:
- snapshots: bfloat16 [1024, 3, 131072], P('tm', None, 'space'), may hold values from -12 to 12
- cell_weights: float32 [131072], P('space'), may hold values from 0.2 to 5
- freq_order: int32 [32], replicated, may hold values from 0 to 31, each once
Outputs:
- energies: float32 [32, 4], P('tm')
- modes: bfloat16 [32, 4, 2, 3, 131072], P('tm', None, None, None, 'space')
All inputs are finite; a program needn't handle non-finite values.
Results may differ from a plain program's by a relative error of at most 0.0043.
Values may be sent and summed in bfloat16 or wider, within the bound.
A program may use at most 192 MiB of HBM per device.

v0:
```python
import functools
import math

import jax
import jax.numpy as jnp
import numpy as np
from jax import lax
from jax.experimental import pallas as pl
from jax.experimental.pallas import tpu as pltpu
from jax.sharding import PartitionSpec as P

NFFT = 64
COMP = 3
MODES = 4
SWEEPS = 3
HALF = 32
NF = 32
NB = 31
SHIFT = 0.61
MESH = pl.DeviceIdType.MESH

CYCLE = (0, 1, 2, 3)
PEERS = [
    (CYCLE[(turn + lead) % 4], dx, dc)
    for dc in (0, 1)
    for turn in range(4)
    for dx, lead in ((2, 0), (1, 1), (3, 3), (0, 2))
    if (CYCLE[(turn + lead) % 4], dx, dc) != (0, 0, 0)
]
GROUPS = 8
IN_GROUP = NF // GROUPS
GROUP_ROWS = IN_GROUP * 2 * HALF
GROUP_ORDER = (0, 2, 6, 4, 1, 3, 7, 5)


def peer_of(me, offset):
    z, x, core = me // 8, (me // 2) % 4, me % 2
    return (((z + offset[0]) % 4) * 4 + (x + offset[1]) % 4) * 2 + (core + offset[2]) % 2


def basis_rows():
    sample = np.arange(NFFT)
    freqs = np.arange(NF)
    turn = ((freqs[:, None] * sample[None, :]) % NFFT).astype(np.float32)
    angle = np.float32(2.0 * math.pi) * turn / np.float32(NFFT)
    hann_angle = np.float32(2.0 * math.pi) * sample.astype(np.float32) / np.float32(NFFT)
    hann = np.float32(0.5) - np.float32(0.5) * np.cos(hann_angle)
    basis = np.stack([hann * np.cos(angle), -hann * np.sin(angle)], 1)
    even = np.concatenate([basis, basis], 2)
    odd = np.concatenate([basis[:, :, HALF:], basis, basis[:, :, :HALF]], 2)
    table = np.zeros((NF, 8, 128), np.float32)
    table[:, 0:2] = even
    table[:, 2:4] = odd
    return table, float(np.sum(hann * hann))


def first_vectors():
    rows = np.arange(NB, dtype=np.float32)[:, None] + np.float32(1.0)
    cols = np.arange(MODES, dtype=np.float32)[None, :] + np.float32(1.0)
    table = np.zeros((2 * HALF, 128), np.float32)
    table[:NB, :MODES] = np.cos(np.float32(SHIFT) * rows * cols)
    return table


def turned(y):
    return jnp.concatenate([y[HALF:], -y[:HALF]], axis=0)


def lane_halves_swapped(x, lane):
    return jnp.where(lane < HALF, pltpu.roll(x, 128 - HALF, 1), pltpu.roll(x, HALF, 1))


def kernel(
    parts, width, scale, factor,
    order, snaps, weights, table, start, energies, modes,
    x_buf, dft, spec, gram, gram_out, gram_in, total, mix, out_buf,
    x_send, x_recv, g_send, g_recv, y_send, y_recv, m_send, m_recv, o_send, o_recv,
):
    me = lax.axis_index("tm")
    row = lax.axis_index("space")
    n_space = lax.axis_size("space")
    own = parts * width

    barrier = pltpu.get_barrier_semaphore()
    for offset in PEERS:
        pl.semaphore_signal(
            barrier, inc=1, device_id={"tm": peer_of(me, offset)}, device_id_type=MESH
        )
    for step in range(1, n_space):
        pl.semaphore_signal(
            barrier, inc=1, device_id={"space": lax.rem(row + step, n_space)}, device_id_type=MESH
        )
    pl.semaphore_wait(barrier, len(PEERS) + n_space - 1)

    def source(owner, part):
        at = pl.multiple_of(owner * own + part * width, width)
        return snaps.at[:, :, pl.ds(at, width)]

    def landing(part, chunk):
        return x_buf.at[part, :, pl.ds(pl.multiple_of(chunk * HALF, HALF), HALF), :]

    @pl.loop(0, parts)
    def _(part):
        for offset in PEERS:
            peer = peer_of(me, offset)
            pltpu.make_async_remote_copy(
                source(peer, part), landing(part, me), x_send.at[part], x_recv.at[part],
                device_id={"tm": peer}, device_id_type=MESH,
            ).start()
        pltpu.make_async_copy(source(me, part), landing(part, me), x_recv.at[part]).start()

    block = lax.broadcasted_iota(jnp.int32, (HALF, 1024), 0)
    chunk = lax.broadcasted_iota(jnp.int32, (HALF, 1024), 1) // HALF
    inside = ((block == chunk) | (block == chunk - 1)) & (block < NB)
    use_even = inside & (block % 2 == 0)
    use_odd = inside & (block % 2 == 1)

    @pl.loop(0, NF)
    def _(j):
        rows = table[order[j]]
        for r in range(2):
            even = jnp.broadcast_to(jnp.tile(rows[r : r + 1], (1, 8)), (HALF, 1024))
            odd = jnp.broadcast_to(jnp.tile(rows[r + 2 : r + 3], (1, 8)), (HALF, 1024))
            band = jnp.where(use_even, even, jnp.where(use_odd, odd, 0.0))
            at = pl.multiple_of(j * NFFT + r * HALF, HALF)
            dft[pl.ds(at, HALF), :] = band.astype(jnp.bfloat16)

    gram[...] = jnp.zeros_like(gram)

    @pl.loop(0, parts)
    def _(part):
        pltpu.make_async_copy(x_buf.at[part], x_buf.at[part], x_recv.at[part]).wait()
        scales = weights[pl.ds(part, 1), :]

        @pl.loop(0, GROUPS)
        def _(g):
            lines = dft[pl.ds(pl.multiple_of(g * GROUP_ROWS, GROUP_ROWS), GROUP_ROWS), :]
            products = gram[g]
            for c in range(COMP):
                found = jnp.dot(lines, x_buf[part, c], preferred_element_type=jnp.float32)
                found = found.astype(jnp.bfloat16)
                spec[g, part, c] = found
                heavy = (found.astype(jnp.float32) * scales).astype(jnp.bfloat16)
                products += lax.dot_general(
                    heavy, found, (((1,), (1,)), ((), ())), preferred_element_type=jnp.float32
                )
            gram[g] = products

    lane = lax.broadcasted_iota(jnp.int32, (HALF, 128), 1)
    low = lane < NFFT
    half_low = low[: HALF // 2]

    @pl.loop(0, GROUPS)
    def _(g):
        for f in range(IN_GROUP):
            tile = gram[g, f * NFFT : (f + 1) * NFFT, (f // 2) * 128 : (f // 2 + 1) * 128]
            if f % 2:
                tile = pltpu.roll(tile, NFFT, 1)
            first, second = tile[:HALF], lane_halves_swapped(tile[HALF:], lane)
            both = first + jnp.where(lane < HALF, second, -second)
            gram_out[g * IN_GROUP + f] = jnp.where(
                half_low, both[: HALF // 2], pltpu.roll(both[HALF // 2 :], NFFT, 1)
            )

    for offset in PEERS:
        peer = peer_of(me, offset)
        pltpu.make_async_remote_copy(
            gram_out.at[peer], gram_in.at[me], g_send, g_recv,
            device_id={"tm": peer}, device_id_type=MESH,
        ).start()
    pltpu.make_async_copy(gram_out.at[me], gram_in.at[me], g_recv).start()
    pltpu.make_async_copy(gram_in, gram_in, g_recv).wait()
    total[row] = jnp.sum(gram_in[...], axis=0)
    for step in range(1, n_space):
        pltpu.make_async_remote_copy(
            total.at[row], total.at[row], y_send, y_recv,
            device_id={"space": lax.rem(row + step, n_space)}, device_id_type=MESH,
        ).start()
    others = total.at[pl.ds(0, n_space - 1)]
    pltpu.make_async_copy(others, others, y_recv).wait()
    packed = total[0]
    for step in range(1, n_space):
        packed = packed + total[step]
    packed = packed * scale

    near = jnp.concatenate([packed, pltpu.roll(packed, NFFT, 1)], axis=0)
    near = jnp.where(low, near, 0.0)
    top = jnp.where(lane < HALF, near, -near)
    bottom = jnp.where(low, lane_halves_swapped(near, lane), 0.0)
    matrix = jnp.concatenate([top, bottom], axis=0)
    empty = jnp.zeros((NFFT, 128), jnp.float32)
    column = lax.broadcasted_iota(jnp.int32, (NFFT, 128), 1)

    def applied(v):
        return jnp.dot(
            matrix, jnp.concatenate([v, empty], axis=0),
            precision=lax.Precision.HIGHEST, preferred_element_type=jnp.float32,
        )

    vec = start[...]
    for _ in range(SWEEPS):
        vec = applied(vec)
        for k in range(MODES):
            new = jnp.broadcast_to(vec[:, k : k + 1], (NFFT, 128))
            new = new / jnp.sqrt(jnp.sum(new * new, axis=0, keepdims=True))
            inner_re = jnp.sum(new * vec, axis=0, keepdims=True)
            inner_im = jnp.sum(new * turned(vec), axis=0, keepdims=True)
            less = vec - (inner_re * new - inner_im * turned(new))
            vec = jnp.where(column == k, new, jnp.where(column > k, less, vec))
    vec = jnp.where(column < MODES, vec, 0.0)

    wide = lax.broadcasted_iota(jnp.int32, (8, 128), 1)
    high = lax.broadcasted_iota(jnp.int32, (8, 128), 0)
    flat = jnp.concatenate([vec * factor, empty], axis=0).T[:8]
    real_rows = jnp.where(wide < HALF, flat, -flat)
    imag_rows = jnp.where(wide < NFFT, lane_halves_swapped(flat, wide), 0.0)
    lines = jnp.where(high < MODES, real_rows, pltpu.roll(imag_rows, MODES, 0))
    place = lax.rem(me, IN_GROUP)
    lines = jnp.where(lax.rem(place, 2) == 1, pltpu.roll(lines, NFFT, 1), lines)
    zero = jnp.zeros_like(lines)
    lines = jnp.concatenate(
        [jnp.where(place < 2, lines, zero), jnp.where(place < 2, zero, lines)], axis=1
    )

    mix[me] = lines
    for offset in PEERS:
        pltpu.make_async_remote_copy(
            mix.at[me], mix.at[me], m_send, m_recv,
            device_id={"tm": peer_of(me, offset)}, device_id_type=MESH,
        ).start()
    energies[...] = jnp.broadcast_to(jnp.sum(vec * applied(vec), axis=0, keepdims=True), (8, 128))
    others = mix.at[pl.ds(0, NF - 1)]
    pltpu.make_async_copy(others, others, m_recv).wait()

    span = pl.ds(pl.multiple_of(me * own, own), own)
    for step in GROUP_ORDER:
        g = lax.rem(me // IN_GROUP + step, GROUPS)
        rows = mix[pl.ds(g * IN_GROUP, IN_GROUP)].reshape(IN_GROUP * 8, GROUP_ROWS)
        rows = rows.astype(jnp.bfloat16)
        for part in range(parts):
            for c in range(COMP):
                made = jnp.dot(rows, spec[g, part, c], preferred_element_type=jnp.float32)
                for f in range(IN_GROUP):
                    out_buf[g * IN_GROUP + f, c, :, part * width : (part + 1) * width] = made[
                        f * 8 : (f + 1) * 8
                    ].astype(jnp.bfloat16)
        for f in range(IN_GROUP):
            j = g * IN_GROUP + f

            @pl.when(j != me)
            def _():
                pltpu.make_async_remote_copy(
                    out_buf.at[j], modes.at[:, :, span], o_send, o_recv,
                    device_id={"tm": j}, device_id_type=MESH,
                ).start()

            @pl.when(j == me)
            def _():
                pltpu.make_async_copy(out_buf.at[j], modes.at[:, :, span], o_recv).start()

    sent = x_buf.at[:, :, pl.ds(0, (NF - 1) * HALF), :]
    for part in range(parts):
        pltpu.make_async_copy(sent.at[part], sent.at[part], x_send.at[part]).wait()
    others = gram_out.at[pl.ds(0, NF - 1)]
    pltpu.make_async_copy(others, others, g_send).wait()
    others = total.at[pl.ds(0, n_space - 1)]
    pltpu.make_async_copy(others, others, y_send).wait()
    others = mix.at[pl.ds(0, NF - 1)]
    pltpu.make_async_copy(others, others, m_send).wait()
    others = out_buf.at[pl.ds(0, NF - 1)]
    pltpu.make_async_copy(others, others, o_send).wait()
    pltpu.make_async_copy(out_buf, out_buf, o_recv).wait()


def per_device(table, energy_sum, snapshots, cell_weights, freq_order):
    n_tm = lax.axis_size("tm")
    cells = snapshots.shape[2]
    own = cells // n_tm
    parts = 4
    width = own // parts
    scale = 1.0 / (energy_sum * COMP * cells * lax.axis_size("space"))
    factor = 1.0 / math.sqrt(energy_sum)
    snaps = jnp.transpose(snapshots, (1, 0, 2))
    weights = lax.dynamic_slice_in_dim(cell_weights, lax.axis_index("tm") * own, own)
    weights = weights.reshape(parts, width)
    dma = pltpu.SemaphoreType.DMA
    vmem = pl.BlockSpec(memory_space=pltpu.VMEM)
    energies, modes = pl.pallas_call(
        functools.partial(kernel, parts, width, scale, factor),
        out_shape=(
            jax.ShapeDtypeStruct((8, 128), jnp.float32),
            jax.ShapeDtypeStruct((COMP, 2 * MODES, cells), jnp.bfloat16),
        ),
        in_specs=[
            pl.BlockSpec(memory_space=pltpu.SMEM),
            pl.BlockSpec(memory_space=pl.ANY),
            vmem,
            vmem,
            vmem,
        ],
        out_specs=(vmem, pl.BlockSpec(memory_space=pl.ANY)),
        scratch_shapes=[
            pltpu.VMEM((parts, COMP, n_tm * HALF, width), jnp.bfloat16),
            pltpu.VMEM((NF * NFFT, n_tm * HALF), jnp.bfloat16),
            pltpu.VMEM((GROUPS, parts, COMP, GROUP_ROWS, width), jnp.bfloat16),
            pltpu.VMEM((GROUPS, GROUP_ROWS, GROUP_ROWS), jnp.float32),
            pltpu.VMEM((NF, HALF // 2, 128), jnp.float32),
            pltpu.VMEM((n_tm, HALF // 2, 128), jnp.float32),
            pltpu.VMEM((lax.axis_size("space"), HALF // 2, 128), jnp.float32),
            pltpu.VMEM((NF, 2 * MODES, GROUP_ROWS), jnp.float32),
            pltpu.VMEM((NF, COMP, 2 * MODES, own), jnp.bfloat16),
            dma((parts,)),
            dma((parts,)),
            dma,
            dma,
            dma,
            dma,
            dma,
            dma,
            dma,
            dma,
        ],
        compiler_params=pltpu.CompilerParams(
            collective_id=0, has_side_effects=True, vmem_limit_bytes=56 << 20
        ),
        name="spod",
    )(freq_order, snaps, weights, table, first_vectors())
    modes = modes.reshape(COMP, 2, MODES, cells).transpose(2, 1, 0, 3)
    return energies[:1, :MODES], modes[None]


def solution(mesh):
    table, energy_sum = basis_rows()
    rounded = table.astype(jnp.bfloat16).astype(np.float32)
    return jax.shard_map(
        functools.partial(per_device, rounded, energy_sum),
        mesh=mesh,
        in_specs=(P("tm", None, "space"), P("space"), P()),
        out_specs=(P("tm", None), P("tm", None, None, None, "space")),
        check_vma=False,
    )
```

profile of v0, /device:TPU:1, one launch (start us, length us, event | category | flops | bytes accessed | tf_op | source)
XLA Modules:
  0.0 139.8 jit_solution(8991921720348038881)
XLA Ops:
  0.6 0.7 dynamic_slice.3
  1.3 0.6 reshape.10.weights
  1.9 131.4 %spod.1 = (f32[8,128]{1,0:T(8,128)}, bf16[3,8,32768]{2,1,0:T(8,128)(2,1)}) custom-call(s32[32]{0:T(128)} %order.1, bf16[3,32,32768]{2,1,0:T(8,128)(2,1)} %bitcast.6, f32[4,256]{1,0:T(4,128)} %reshape.10.weights, f32[32,8,128]{2,1,0:T(8,128)} %constant.16.clone.table, f32[64,128]{1,0:T(8,128)} %constant.17.clone.start), custom_call_target="tpu_custom_call" | custom-call | tf_op jit(solution)/shard_map/spod/pallas_call | solution.py:288
  133.3 1.2 slice.3
  134.5 2.5 %reshape.11 = bf16[3,2,4,32768]{3,2,1,0:T(4,128)(2,1)S(1)} reshape(bf16[3,8,32768]{2,1,0:T(8,128)(2,1)} %get-tuple-element.5) | data formatting | bytes 3145728 | tf_op jit(solution)/shard_map/reshape | solution.py:328
  137.0 2.8 %copy.9 = bf16[3,2,4,32768]{3,1,0,2:T(2,128)(2,1)} copy(bf16[3,2,4,32768]{3,2,1,0:T(4,128)(2,1)S(1)} %reshape.11) | data formatting | bytes 3145728 | tf_op jit(solution)/shard_map/reshape | solution.py:328
where the time goes:
time: 141 us; the launch traced here: 140 us
  Pallas kernels  131 us (93%)
  local copies, waits for them, and re-layouts  7.73 us (5%)
    pallas_call x1, Pallas kernels, per_device(): pl.pallas_call(functools.partial(kernel, parts, width, scale, factor), ou...  131 us
    reshape x2, local copies, waits for them, and re-layouts, per_device(): modes = modes.reshape(COMP, 2, MODES, cells).transpose(2, 1, 0, 3)  5.24 us

commit v1 on v0

--- a/solution.py
+++ b/solution.py
@@ -30,7 +30,11 @@
 GROUPS = 8
 IN_GROUP = NF // GROUPS
 GROUP_ROWS = IN_GROUP * 2 * HALF
-GROUP_ORDER = (0, 2, 6, 4, 1, 3, 7, 5)
+GROUP_ORDER = (4, 5, 3, 2, 6, 7, 1, 0)
+STRIP = 8 * HALF
+STRIPS = 4
+STEP_ROWS = 8 * NFFT
+BAND_ROWS = 9 * NFFT
 
 
 def peer_of(me, offset):
@@ -73,8 +77,8 @@
 def kernel(
     parts, width, scale, factor,
     order, snaps, weights, table, start, energies, modes,
-    x_buf, dft, spec, gram, gram_out, gram_in, total, mix, out_buf,
-    x_send, x_recv, g_send, g_recv, y_send, y_recv, m_send, m_recv, o_send, o_recv,
+    x_buf, w_buf, lines_buf, dft, fresh, spec, gram, gram_out, gram_in, total, mix, out_buf,
+    x_send, x_recv, g_send, g_recv, y_send, y_recv, m_send, m_recv, o_send, o_recv, w_sem,
 ):
     me = lax.axis_index("tm")
     row = lax.axis_index("space")
@@ -109,36 +113,63 @@
             ).start()
         pltpu.make_async_copy(source(me, part), landing(part, me), x_recv.at[part]).start()
 
-    block = lax.broadcasted_iota(jnp.int32, (HALF, 1024), 0)
-    chunk = lax.broadcasted_iota(jnp.int32, (HALF, 1024), 1) // HALF
-    inside = ((block == chunk) | (block == chunk - 1)) & (block < NB)
-    use_even = inside & (block % 2 == 0)
-    use_odd = inside & (block % 2 == 1)
-
-    @pl.loop(0, NF)
-    def _(j):
+    load = pltpu.make_async_copy(weights.at[me], w_buf, w_sem)
+    load.start()
+    for j in range(NF):
         rows = table[order[j]]
-        for r in range(2):
-            even = jnp.broadcast_to(jnp.tile(rows[r : r + 1], (1, 8)), (HALF, 1024))
-            odd = jnp.broadcast_to(jnp.tile(rows[r + 2 : r + 3], (1, 8)), (HALF, 1024))
-            band = jnp.where(use_even, even, jnp.where(use_odd, odd, 0.0))
-            at = pl.multiple_of(j * NFFT + r * HALF, HALF)
-            dft[pl.ds(at, HALF), :] = band.astype(jnp.bfloat16)
+        lines_buf[0, 2 * j : 2 * j + 2] = rows[0:2]
+        lines_buf[1, 2 * j : 2 * j + 2] = rows[2:4]
+    time = lax.broadcasted_iota(jnp.int32, (NFFT, STRIP), 1)
+    for b in range(9):
+        rows = lines_buf[(b - 1) % 2]
+        since = time - HALF * (b - 1)
+        band = jnp.where((since >= 0) & (since < NFFT), jnp.concatenate([rows, rows], axis=1), 0.0)
+        dft[b * NFFT : (b + 1) * NFFT] = band.astype(jnp.bfloat16)
 
     gram[...] = jnp.zeros_like(gram)
+    columns = width // 128
+    fresh[:, NB * NFFT :] = jnp.zeros((COMP * columns, NFFT, 128), jnp.float32)
+    load.wait()
 
     @pl.loop(0, parts)
     def _(part):
         pltpu.make_async_copy(x_buf.at[part], x_buf.at[part], x_recv.at[part]).wait()
-        scales = weights[pl.ds(part, 1), :]
+        scales = jnp.concatenate(
+            [w_buf[pl.ds(part * columns + k, 1), :] for k in range(columns)], axis=1
+        )
+        for c in range(COMP):
+            for strip in range(STRIPS):
+                first = NFFT if strip == 0 else 0
+                last = BAND_ROWS - NFFT if strip == STRIPS - 1 else BAND_ROWS
+                made = jnp.dot(
+                    dft[first:last], x_buf[part, c, strip * STRIP : (strip + 1) * STRIP],
+                    preferred_element_type=jnp.float32,
+                )
+                at = strip * STEP_ROWS
+                for k in range(columns):
+                    piece = made[:, k * 128 : (k + 1) * 128]
+                    if strip:
+                        fresh[c * columns + k, at - NFFT : at] += piece[:NFFT]
+                        piece = piece[NFFT:]
+                    fresh[c * columns + k, at : at + piece.shape[0]] = piece
 
         @pl.loop(0, GROUPS)
         def _(g):
-            lines = dft[pl.ds(pl.multiple_of(g * GROUP_ROWS, GROUP_ROWS), GROUP_ROWS), :]
             products = gram[g]
             for c in range(COMP):
-                found = jnp.dot(lines, x_buf[part, c], preferred_element_type=jnp.float32)
-                found = found.astype(jnp.bfloat16)
+                found = jnp.concatenate(
+                    [
+                        jnp.concatenate(
+                            [
+                                fresh[c * columns + k, pl.ds(g * 8 + line, HALF, stride=NFFT), :]
+                                for line in range(8)
+                            ],
+                            axis=0,
+                        )
+                        for k in range(columns)
+                    ],
+                    axis=1,
+                ).astype(jnp.bfloat16)
                 spec[g, part, c] = found
                 heavy = (found.astype(jnp.float32) * scales).astype(jnp.bfloat16)
                 products += lax.dot_general(
@@ -210,40 +241,44 @@
     vec = jnp.where(column < MODES, vec, 0.0)
 
     wide = lax.broadcasted_iota(jnp.int32, (8, 128), 1)
-    high = lax.broadcasted_iota(jnp.int32, (8, 128), 0)
     flat = jnp.concatenate([vec * factor, empty], axis=0).T[:8]
     real_rows = jnp.where(wide < HALF, flat, -flat)
     imag_rows = jnp.where(wide < NFFT, lane_halves_swapped(flat, wide), 0.0)
-    lines = jnp.where(high < MODES, real_rows, pltpu.roll(imag_rows, MODES, 0))
-    place = lax.rem(me, IN_GROUP)
-    lines = jnp.where(lax.rem(place, 2) == 1, pltpu.roll(lines, NFFT, 1), lines)
-    zero = jnp.zeros_like(lines)
     lines = jnp.concatenate(
-        [jnp.where(place < 2, lines, zero), jnp.where(place < 2, zero, lines)], axis=1
+        [rows[k : k + 1] for k in range(MODES) for rows in (real_rows, imag_rows)], axis=0
     )
-
-    mix[me] = lines
+    lines = jnp.where(lax.rem(me, 2) == 1, pltpu.roll(lines, NFFT, 1), lines)
+
+    mix[me] = lines.astype(jnp.bfloat16)
     for offset in PEERS:
         pltpu.make_async_remote_copy(
             mix.at[me], mix.at[me], m_send, m_recv,
             device_id={"tm": peer_of(me, offset)}, device_id_type=MESH,
         ).start()
-    energies[...] = jnp.broadcast_to(jnp.sum(vec * applied(vec), axis=0, keepdims=True), (8, 128))
+    energies[...] = jnp.sum(vec * applied(vec), axis=0, keepdims=True)[:, :MODES]
     others = mix.at[pl.ds(0, NF - 1)]
     pltpu.make_async_copy(others, others, m_recv).wait()
 
     span = pl.ds(pl.multiple_of(me * own, own), own)
     for step in GROUP_ORDER:
         g = lax.rem(me // IN_GROUP + step, GROUPS)
-        rows = mix[pl.ds(g * IN_GROUP, IN_GROUP)].reshape(IN_GROUP * 8, GROUP_ROWS)
-        rows = rows.astype(jnp.bfloat16)
+        zero = jnp.zeros((8, 128), jnp.float32)
+        rows = [mix[g * IN_GROUP + f].astype(jnp.float32) for f in range(IN_GROUP)]
+        rows = [
+            jnp.concatenate([line, zero] if f < 2 else [zero, line], axis=1)
+            for f, line in enumerate(rows)
+        ]
+        rows = jnp.concatenate(rows, axis=0).astype(jnp.bfloat16)
         for part in range(parts):
             for c in range(COMP):
                 made = jnp.dot(rows, spec[g, part, c], preferred_element_type=jnp.float32)
+                made = made.astype(jnp.bfloat16)
+                here = slice(part * width, (part + 1) * width)
                 for f in range(IN_GROUP):
-                    out_buf[g * IN_GROUP + f, c, :, part * width : (part + 1) * width] = made[
-                        f * 8 : (f + 1) * 8
-                    ].astype(jnp.bfloat16)
+                    for k in range(MODES):
+                        out_buf[g * IN_GROUP + f, k * COMP + c, :, here] = made[
+                            f * 8 + 2 * k : f * 8 + 2 * k + 2
+                        ]
         for f in range(IN_GROUP):
             j = g * IN_GROUP + f
 
@@ -281,36 +316,39 @@
     scale = 1.0 / (energy_sum * COMP * cells * lax.axis_size("space"))
     factor = 1.0 / math.sqrt(energy_sum)
     snaps = jnp.transpose(snapshots, (1, 0, 2))
-    weights = lax.dynamic_slice_in_dim(cell_weights, lax.axis_index("tm") * own, own)
-    weights = weights.reshape(parts, width)
+    weights = cell_weights.reshape(n_tm, own // 128, 128)
     dma = pltpu.SemaphoreType.DMA
     vmem = pl.BlockSpec(memory_space=pltpu.VMEM)
     energies, modes = pl.pallas_call(
         functools.partial(kernel, parts, width, scale, factor),
         out_shape=(
-            jax.ShapeDtypeStruct((8, 128), jnp.float32),
-            jax.ShapeDtypeStruct((COMP, 2 * MODES, cells), jnp.bfloat16),
+            jax.ShapeDtypeStruct((1, MODES), jnp.float32),
+            jax.ShapeDtypeStruct((MODES * COMP, 2, cells), jnp.bfloat16),
         ),
         in_specs=[
             pl.BlockSpec(memory_space=pltpu.SMEM),
             pl.BlockSpec(memory_space=pl.ANY),
-            vmem,
+            pl.BlockSpec(memory_space=pl.ANY),
             vmem,
             vmem,
         ],
         out_specs=(vmem, pl.BlockSpec(memory_space=pl.ANY)),
         scratch_shapes=[
             pltpu.VMEM((parts, COMP, n_tm * HALF, width), jnp.bfloat16),
-            pltpu.VMEM((NF * NFFT, n_tm * HALF), jnp.bfloat16),
+            pltpu.VMEM((own // 128, 128), jnp.float32),
+            pltpu.VMEM((2, NFFT, 128), jnp.float32),
+            pltpu.VMEM((BAND_ROWS, STRIP), jnp.bfloat16),
+            pltpu.VMEM((COMP * width // 128, NF * NFFT, 128), jnp.float32),
             pltpu.VMEM((GROUPS, parts, COMP, GROUP_ROWS, width), jnp.bfloat16),
             pltpu.VMEM((GROUPS, GROUP_ROWS, GROUP_ROWS), jnp.float32),
             pltpu.VMEM((NF, HALF // 2, 128), jnp.float32),
             pltpu.VMEM((n_tm, HALF // 2, 128), jnp.float32),
             pltpu.VMEM((lax.axis_size("space"), HALF // 2, 128), jnp.float32),
-            pltpu.VMEM((NF, 2 * MODES, GROUP_ROWS), jnp.float32),
-            pltpu.VMEM((NF, COMP, 2 * MODES, own), jnp.bfloat16),
+            pltpu.VMEM((NF, 2 * MODES, 128), jnp.bfloat16),
+            pltpu.VMEM((NF, MODES * COMP, 2, own), jnp.bfloat16),
             dma((parts,)),
             dma((parts,)),
+            dma,
             dma,
             dma,
             dma,
@@ -325,8 +363,8 @@
         ),
         name="spod",
     )(freq_order, snaps, weights, table, first_vectors())
-    modes = modes.reshape(COMP, 2, MODES, cells).transpose(2, 1, 0, 3)
-    return energies[:1, :MODES], modes[None]
+    modes = modes.reshape(MODES, COMP, 2, cells).transpose(0, 2, 1, 3)
+    return energies, modes[None]
 
 
 def solution(mesh):

time: 141 us -> 136 us (0.965)
  local copies, waits for them, and re-layouts: 7.73 us -> 5.05 us
    reshape x3 -> x0, local copies, waits for them, and re-layouts: 5.85 us -> none  [the longest x2 5.24 us: per_device(): modes = modes.reshape(COMP, 2, MODES, cells).transpose(2, 1, 0, 3)]
    unnamed x0 -> x2, local copies, waits for them, and re-layouts: none -> 5.05 us
where the time goes in v1:
time: 136 us
  Pallas kernels  130 us (96%)
  local copies, waits for them, and re-layouts  5.05 us (4%)
    pallas_call x1, Pallas kernels, per_device(): pl.pallas_call(functools.partial(kernel, parts, width, scale, factor), ou...  130 us
    unnamed x2, local copies, waits for them, and re-layouts  5.05 us

profile of v1, /device:TPU:1, one launch (start us, length us, event | category | flops | bytes accessed | tf_op | source)
XLA Modules:
  0.0 135.8 jit_solution(10331615633159053014)
XLA Ops:
  0.6 130.1 %spod.1 = (f32[1,4]{1,0:T(1,128)}, bf16[12,2,32768]{2,1,0:T(2,128)(2,1)}) custom-call(s32[32]{0:T(128)} %order.1, bf16[3,32,32768]{2,1,0:T(8,128)(2,1)} %bitcast.7, f32[32,8,128]{2,1,0:T(8,128)} %bitcast.9, f32[32,8,128]{2,1,0:T(8,128)} %constant.4.clone.table, f32[64,128]{1,0:T(8,128)} %constant.5.clone.start), custom_call_target="tpu_custom_call" | custom-call | tf_op jit(solution)/shard_map/spod/pallas_call | solution.py:322
  130.7 1.2 copy.9
  131.9 3.9 %copy.10 = bf16[1,4,2,3,32768]{4,2,3,1,0:T(2,128)(2,1)} copy(bf16[1,4,2,3,32768]{4,2,3,1,0:T(2,128)(2,1)} %bitcast.8) | data formatting | bytes 3145728

commit v2 on v1

--- a/solution.py
+++ b/solution.py
@@ -33,8 +33,7 @@
 GROUP_ORDER = (4, 5, 3, 2, 6, 7, 1, 0)
 STRIP = 8 * HALF
 STRIPS = 4
-STEP_ROWS = 8 * NFFT
-BAND_ROWS = 9 * NFFT
+STRIP_ROWS = 8 * 2 * NF
 
 
 def peer_of(me, offset):
@@ -77,7 +76,7 @@
 def kernel(
     parts, width, scale, factor,
     order, snaps, weights, table, start, energies, modes,
-    x_buf, w_buf, lines_buf, dft, fresh, spec, gram, gram_out, gram_in, total, mix, out_buf,
+    x_buf, w_buf, dft, dft_end, fresh, spec, gram, gram_out, gram_in, total, mix, out_buf,
     x_send, x_recv, g_send, g_recv, y_send, y_recv, m_send, m_recv, o_send, o_recv, w_sem,
 ):
     me = lax.axis_index("tm")
@@ -115,20 +114,28 @@
 
     load = pltpu.make_async_copy(weights.at[me], w_buf, w_sem)
     load.start()
-    for j in range(NF):
+    block = lax.broadcasted_iota(jnp.int32, (8, 2 * STRIP), 0)
+    since = lax.broadcasted_iota(jnp.int32, (8, 2 * STRIP), 1) - HALF * block
+    inside = (since >= 0) & (since < NFFT)
+    use_even = inside & (block % 2 == 0)
+    use_odd = inside & (block % 2 == 1)
+    present = (block < 7)[:, :STRIP]
+
+    @pl.loop(0, NF)
+    def _(j):
         rows = table[order[j]]
-        lines_buf[0, 2 * j : 2 * j + 2] = rows[0:2]
-        lines_buf[1, 2 * j : 2 * j + 2] = rows[2:4]
-    time = lax.broadcasted_iota(jnp.int32, (NFFT, STRIP), 1)
-    for b in range(9):
-        rows = lines_buf[(b - 1) % 2]
-        since = time - HALF * (b - 1)
-        band = jnp.where((since >= 0) & (since < NFFT), jnp.concatenate([rows, rows], axis=1), 0.0)
-        dft[b * NFFT : (b + 1) * NFFT] = band.astype(jnp.bfloat16)
+        bands = []
+        for r in range(2):
+            even = jnp.broadcast_to(jnp.tile(rows[r : r + 1], (1, 4)), (8, 2 * STRIP))
+            odd = jnp.broadcast_to(jnp.tile(rows[r + 2 : r + 3], (1, 4)), (8, 2 * STRIP))
+            bands.append(jnp.where(use_even, even, jnp.where(use_odd, odd, 0.0)))
+        at = pl.ds(pl.multiple_of(j * 16, 16), 16)
+        dft[at, :] = jnp.concatenate(bands, axis=0).astype(jnp.bfloat16)
+        bands = [jnp.where(present, band[:, :STRIP], 0.0) for band in bands]
+        dft_end[at, :] = jnp.concatenate(bands, axis=0).astype(jnp.bfloat16)
 
     gram[...] = jnp.zeros_like(gram)
     columns = width // 128
-    fresh[:, NB * NFFT :] = jnp.zeros((COMP * columns, NFFT, 128), jnp.float32)
     load.wait()
 
     @pl.loop(0, parts)
@@ -139,36 +146,24 @@
         )
         for c in range(COMP):
             for strip in range(STRIPS):
-                first = NFFT if strip == 0 else 0
-                last = BAND_ROWS - NFFT if strip == STRIPS - 1 else BAND_ROWS
-                made = jnp.dot(
-                    dft[first:last], x_buf[part, c, strip * STRIP : (strip + 1) * STRIP],
+                last = strip == STRIPS - 1
+                rows = slice(strip * STRIP, (strip + 1 if last else strip + 2) * STRIP)
+                fresh[c, strip] = jnp.dot(
+                    (dft_end if last else dft)[...], x_buf[part, c, rows],
                     preferred_element_type=jnp.float32,
                 )
-                at = strip * STEP_ROWS
-                for k in range(columns):
-                    piece = made[:, k * 128 : (k + 1) * 128]
-                    if strip:
-                        fresh[c * columns + k, at - NFFT : at] += piece[:NFFT]
-                        piece = piece[NFFT:]
-                    fresh[c * columns + k, at : at + piece.shape[0]] = piece
 
         @pl.loop(0, GROUPS)
         def _(g):
             products = gram[g]
             for c in range(COMP):
+                pieces = [
+                    fresh[c, strip, pl.ds(pl.multiple_of(g * 64, 64), 64), :]
+                    for strip in range(STRIPS)
+                ]
                 found = jnp.concatenate(
-                    [
-                        jnp.concatenate(
-                            [
-                                fresh[c * columns + k, pl.ds(g * 8 + line, HALF, stride=NFFT), :]
-                                for line in range(8)
-                            ],
-                            axis=0,
-                        )
-                        for k in range(columns)
-                    ],
-                    axis=1,
+                    [piece[line * 8 : line * 8 + 8] for line in range(8) for piece in pieces],
+                    axis=0,
                 ).astype(jnp.bfloat16)
                 spec[g, part, c] = found
                 heavy = (found.astype(jnp.float32) * scales).astype(jnp.bfloat16)
@@ -305,6 +300,20 @@
     others = out_buf.at[pl.ds(0, NF - 1)]
     pltpu.make_async_copy(others, others, o_send).wait()
     pltpu.make_async_copy(out_buf, out_buf, o_recv).wait()
+
+
+def hand_over(energies, modes, energies_out, modes_out, held, in_sem, out_sem):
+    energies_out[...] = energies[...]
+    rows = range(modes.shape[0])
+    takes = [pltpu.make_async_copy(modes.at[k], held.at[k], in_sem.at[k]) for k in rows]
+    gives = [pltpu.make_async_copy(held.at[k], modes_out.at[k], out_sem.at[k]) for k in rows]
+    for take in takes:
+        take.start()
+    for take, give in zip(takes, gives):
+        take.wait()
+        give.start()
+    for give in gives:
+        give.wait()
 
 
 def per_device(table, energy_sum, snapshots, cell_weights, freq_order):
@@ -336,9 +345,9 @@
         scratch_shapes=[
             pltpu.VMEM((parts, COMP, n_tm * HALF, width), jnp.bfloat16),
             pltpu.VMEM((own // 128, 128), jnp.float32),
-            pltpu.VMEM((2, NFFT, 128), jnp.float32),
-            pltpu.VMEM((BAND_ROWS, STRIP), jnp.bfloat16),
-            pltpu.VMEM((COMP * width // 128, NF * NFFT, 128), jnp.float32),
+            pltpu.VMEM((STRIP_ROWS, 2 * STRIP), jnp.bfloat16),
+            pltpu.VMEM((STRIP_ROWS, STRIP), jnp.bfloat16),
+            pltpu.VMEM((COMP, STRIPS, STRIP_ROWS, width), jnp.float32),
             pltpu.VMEM((GROUPS, parts, COMP, GROUP_ROWS, width), jnp.bfloat16),
             pltpu.VMEM((GROUPS, GROUP_ROWS, GROUP_ROWS), jnp.float32),
             pltpu.VMEM((NF, HALF // 2, 128), jnp.float32),
@@ -363,6 +372,21 @@
         ),
         name="spod",
     )(freq_order, snaps, weights, table, first_vectors())
+    energies, modes = pl.pallas_call(
+        hand_over,
+        out_shape=(
+            jax.ShapeDtypeStruct(energies.shape, energies.dtype),
+            jax.ShapeDtypeStruct(modes.shape, modes.dtype),
+        ),
+        in_specs=[vmem, pl.BlockSpec(memory_space=pl.ANY)],
+        out_specs=(vmem, pl.BlockSpec(memory_space=pl.ANY)),
+        scratch_shapes=[
+            pltpu.VMEM(modes.shape, modes.dtype),
+            dma((MODES * COMP,)),
+            dma((MODES * COMP,)),
+        ],
+        name="hand_over",
+    )(energies, modes)
     modes = modes.reshape(MODES, COMP, 2, cells).transpose(0, 2, 1, 3)
     return energies, modes[None]
 

time: 136 us -> 131 us (0.963)
  local copies, waits for them, and re-layouts: 5.05 us -> 0 us
    unnamed x2 -> x0, local copies, waits for them, and re-layouts: 5.05 us -> none
    pallas_call x1, Pallas kernels: 130 us -> 126 us  [per_device(): pl.pallas_call(functools.partial(kernel, parts, width, scale, factor), ou...]
    pallas_call x0 -> x1, Pallas kernels: none -> 3.46 us  [per_device(): pl.pallas_call(hand_over, out_shape=(jax.ShapeDtypeStruct(energies.shape,...]
where the time goes in v2:
time: 131 us; the launch traced here: 130 us
  Pallas kernels  130 us (99%)
    pallas_call x1, Pallas kernels, per_device(): pl.pallas_call(functools.partial(kernel, parts, width, scale, factor), ou...  126 us
    pallas_call x1, Pallas kernels, per_device(): pl.pallas_call(hand_over, out_shape=(jax.ShapeDtypeStruct(energies.shape,...  3.46 us

profile of v2, /device:TPU:1, one launch (start us, length us, event | category | flops | bytes accessed | tf_op | source)
XLA Modules:
  0.0 130.4 jit_solution(12853642743420037062)
XLA Ops:
  0.6 126.3 %spod.1 = (f32[1,4]{1,0:T(1,128)}, bf16[12,2,32768]{2,1,0:T(2,128)(2,1)}) custom-call(s32[32]{0:T(128)} %order.1, bf16[3,32,32768]{2,1,0:T(8,128)(2,1)} %bitcast.7, f32[32,8,128]{2,1,0:T(8,128)} %bitcast.8, f32[32,8,128]{2,1,0:T(8,128)} %constant.4.clone.table, f32[64,128]{1,0:T(8,128)} %constant.5.clone.start), custom_call_target="tpu_custom_call" | custom-call | tf_op jit(solution)/shard_map/spod/pallas_call | solution.py:331
  126.9 3.5 %hand_over.1 = (f32[1,4]{1,0:T(1,128)}, bf16[12,2,32768]{2,1,0:T(2,128)(2,1)}) custom-call(f32[1,4]{1,0:T(1,128)} %get-tuple-element.6.energies, bf16[12,2,32768]{2,1,0:T(2,128)(2,1)} %get-tuple-element.7.modes), custom_call_target="tpu_custom_call" | custom-call | tf_op jit(solution)/shard_map/hand_over/pallas_call | solution.py:375

commit v3 on v2

--- a/solution.py
+++ b/solution.py
@@ -30,7 +30,7 @@
 GROUPS = 8
 IN_GROUP = NF // GROUPS
 GROUP_ROWS = IN_GROUP * 2 * HALF
-GROUP_ORDER = (4, 5, 3, 2, 6, 7, 1, 0)
+GROUP_ORDER = (0, 1, 5, 2, 6, 4, 3, 7)
 STRIP = 8 * HALF
 STRIPS = 4
 STRIP_ROWS = 8 * 2 * NF
@@ -75,14 +75,17 @@
 
 def kernel(
     parts, width, scale, factor,
-    order, snaps, weights, table, start, energies, modes,
-    x_buf, w_buf, dft, dft_end, fresh, spec, gram, gram_out, gram_in, total, mix, out_buf,
-    x_send, x_recv, g_send, g_recv, y_send, y_recv, m_send, m_recv, o_send, o_recv, w_sem,
+    order_far, snaps, weights, table_far, start_far, energies, modes,
+    order, table, start, w_buf, x_buf, dft, dft_end, fresh, spec, gram,
+    gram_out, gram_in, total, mine, mix, out_buf,
+    load_sem, x_send, x_recv, g_send, g_recv, y_send, y_recv, m_send, m_recv, o_send, o_recv,
 ):
     me = lax.axis_index("tm")
     row = lax.axis_index("space")
     n_space = lax.axis_size("space")
     own = parts * width
+    last_part = parts - 1
+    home = me // IN_GROUP
 
     barrier = pltpu.get_barrier_semaphore()
     for offset in PEERS:
@@ -93,6 +96,14 @@
         pl.semaphore_signal(
             barrier, inc=1, device_id={"space": lax.rem(row + step, n_space)}, device_id_type=MESH
         )
+    loads = [
+        pltpu.make_async_copy(far, near, load_sem.at[k])
+        for k, (far, near) in enumerate(
+            ((order_far, order), (table_far, table), (start_far, start), (weights.at[me], w_buf))
+        )
+    ]
+    for load in loads:
+        load.start()
     pl.semaphore_wait(barrier, len(PEERS) + n_space - 1)
 
     def source(owner, part):
@@ -112,14 +123,14 @@
             ).start()
         pltpu.make_async_copy(source(me, part), landing(part, me), x_recv.at[part]).start()
 
-    load = pltpu.make_async_copy(weights.at[me], w_buf, w_sem)
-    load.start()
     block = lax.broadcasted_iota(jnp.int32, (8, 2 * STRIP), 0)
     since = lax.broadcasted_iota(jnp.int32, (8, 2 * STRIP), 1) - HALF * block
     inside = (since >= 0) & (since < NFFT)
     use_even = inside & (block % 2 == 0)
     use_odd = inside & (block % 2 == 1)
     present = (block < 7)[:, :STRIP]
+    for load in loads:
+        load.wait()
 
     @pl.loop(0, NF)
     def _(j):
@@ -135,66 +146,68 @@
         dft_end[at, :] = jnp.concatenate(bands, axis=0).astype(jnp.bfloat16)
 
     gram[...] = jnp.zeros_like(gram)
-    columns = width // 128
-    load.wait()
-
-    @pl.loop(0, parts)
+
+    def transform(part):
+        pltpu.make_async_copy(x_buf.at[part], x_buf.at[part], x_recv.at[part]).wait()
+        for strip in range(STRIPS):
+            last = strip == STRIPS - 1
+            rows = slice(strip * STRIP, (strip + 1 if last else strip + 2) * STRIP)
+            given = jnp.concatenate([x_buf[part, c, rows] for c in range(COMP)], axis=1)
+            fresh[strip] = jnp.dot(
+                (dft_end if last else dft)[...], given, preferred_element_type=jnp.float32
+            )
+
+    def accumulate(part, g):
+        pieces = [fresh[k, pl.ds(pl.multiple_of(g * 64, 64), 64), :] for k in range(STRIPS)]
+        found = jnp.concatenate(
+            [piece[line * 8 : line * 8 + 8] for line in range(8) for piece in pieces], axis=0
+        ).astype(jnp.bfloat16)
+        spec[g, part] = found
+        scales = jnp.tile(w_buf[pl.ds(part, 1), :], (1, COMP))
+        heavy = (found.astype(jnp.float32) * scales).astype(jnp.bfloat16)
+        gram[g] += lax.dot_general(
+            heavy, found, (((1,), (1,)), ((), ())), preferred_element_type=jnp.float32
+        )
+
+    @pl.loop(0, last_part)
     def _(part):
-        pltpu.make_async_copy(x_buf.at[part], x_buf.at[part], x_recv.at[part]).wait()
-        scales = jnp.concatenate(
-            [w_buf[pl.ds(part * columns + k, 1), :] for k in range(columns)], axis=1
-        )
-        for c in range(COMP):
-            for strip in range(STRIPS):
-                last = strip == STRIPS - 1
-                rows = slice(strip * STRIP, (strip + 1 if last else strip + 2) * STRIP)
-                fresh[c, strip] = jnp.dot(
-                    (dft_end if last else dft)[...], x_buf[part, c, rows],
-                    preferred_element_type=jnp.float32,
-                )
+        transform(part)
 
         @pl.loop(0, GROUPS)
         def _(g):
-            products = gram[g]
-            for c in range(COMP):
-                pieces = [
-                    fresh[c, strip, pl.ds(pl.multiple_of(g * 64, 64), 64), :]
-                    for strip in range(STRIPS)
-                ]
-                found = jnp.concatenate(
-                    [piece[line * 8 : line * 8 + 8] for line in range(8) for piece in pieces],
-                    axis=0,
-                ).astype(jnp.bfloat16)
-                spec[g, part, c] = found
-                heavy = (found.astype(jnp.float32) * scales).astype(jnp.bfloat16)
-                products += lax.dot_general(
-                    heavy, found, (((1,), (1,)), ((), ())), preferred_element_type=jnp.float32
-                )
-            gram[g] = products
+            accumulate(part, g)
 
     lane = lax.broadcasted_iota(jnp.int32, (HALF, 128), 1)
     low = lane < NFFT
     half_low = low[: HALF // 2]
+    transform(last_part)
 
     @pl.loop(0, GROUPS)
-    def _(g):
+    def _(step):
+        g = lax.rem(home + step, GROUPS)
+        accumulate(last_part, g)
         for f in range(IN_GROUP):
+            j = g * IN_GROUP + f
             tile = gram[g, f * NFFT : (f + 1) * NFFT, (f // 2) * 128 : (f // 2 + 1) * 128]
             if f % 2:
                 tile = pltpu.roll(tile, NFFT, 1)
             first, second = tile[:HALF], lane_halves_swapped(tile[HALF:], lane)
             both = first + jnp.where(lane < HALF, second, -second)
-            gram_out[g * IN_GROUP + f] = jnp.where(
+            gram_out[j] = jnp.where(
                 half_low, both[: HALF // 2], pltpu.roll(both[HALF // 2 :], NFFT, 1)
             )
 
-    for offset in PEERS:
-        peer = peer_of(me, offset)
-        pltpu.make_async_remote_copy(
-            gram_out.at[peer], gram_in.at[me], g_send, g_recv,
-            device_id={"tm": peer}, device_id_type=MESH,
-        ).start()
-    pltpu.make_async_copy(gram_out.at[me], gram_in.at[me], g_recv).start()
+            @pl.when(j != me)
+            def _():
+                pltpu.make_async_remote_copy(
+                    gram_out.at[j], gram_in.at[me], g_send, g_recv,
+                    device_id={"tm": j}, device_id_type=MESH,
+                ).start()
+
+            @pl.when(j == me)
+            def _():
+                pltpu.make_async_copy(gram_out.at[j], gram_in.at[me], g_recv).start()
+
     pltpu.make_async_copy(gram_in, gram_in, g_recv).wait()
     total[row] = jnp.sum(gram_in[...], axis=0)
     for step in range(1, n_space):
@@ -244,19 +257,20 @@
     )
     lines = jnp.where(lax.rem(me, 2) == 1, pltpu.roll(lines, NFFT, 1), lines)
 
-    mix[me] = lines.astype(jnp.bfloat16)
+    mine[...] = lines.astype(jnp.bfloat16)
     for offset in PEERS:
         pltpu.make_async_remote_copy(
-            mix.at[me], mix.at[me], m_send, m_recv,
+            mine, mix.at[me], m_send, m_recv.at[home],
             device_id={"tm": peer_of(me, offset)}, device_id_type=MESH,
         ).start()
+    pltpu.make_async_copy(mine, mix.at[me], m_recv.at[home]).start()
     energies[...] = jnp.sum(vec * applied(vec), axis=0, keepdims=True)[:, :MODES]
-    others = mix.at[pl.ds(0, NF - 1)]
-    pltpu.make_async_copy(others, others, m_recv).wait()
 
     span = pl.ds(pl.multiple_of(me * own, own), own)
     for step in GROUP_ORDER:
-        g = lax.rem(me // IN_GROUP + step, GROUPS)
+        g = lax.rem(home + step, GROUPS)
+        four = mix.at[pl.ds(g * IN_GROUP, IN_GROUP)]
+        pltpu.make_async_copy(four, four, m_recv.at[g]).wait()
         zero = jnp.zeros((8, 128), jnp.float32)
         rows = [mix[g * IN_GROUP + f].astype(jnp.float32) for f in range(IN_GROUP)]
         rows = [
@@ -265,13 +279,14 @@
         ]
         rows = jnp.concatenate(rows, axis=0).astype(jnp.bfloat16)
         for part in range(parts):
+            made = jnp.dot(rows, spec[g, part], preferred_element_type=jnp.float32)
+            made = made.astype(jnp.bfloat16)
             for c in range(COMP):
-                made = jnp.dot(rows, spec[g, part, c], preferred_element_type=jnp.float32)
-                made = made.astype(jnp.bfloat16)
+                piece = made[:, c * width : (c + 1) * width]
                 here = slice(part * width, (part + 1) * width)
                 for f in range(IN_GROUP):
                     for k in range(MODES):
-                        out_buf[g * IN_GROUP + f, k * COMP + c, :, here] = made[
+                        out_buf[g * IN_GROUP + f, k * COMP + c, :, here] = piece[
                             f * 8 + 2 * k : f * 8 + 2 * k + 2
                         ]
         for f in range(IN_GROUP):
@@ -302,25 +317,18 @@
     pltpu.make_async_copy(out_buf, out_buf, o_recv).wait()
 
 
-def hand_over(energies, modes, energies_out, modes_out, held, in_sem, out_sem):
+def hand_over(energies, modes, energies_out, modes_out, sem):
+    give = pltpu.make_async_copy(modes, modes_out, sem)
+    give.start()
     energies_out[...] = energies[...]
-    rows = range(modes.shape[0])
-    takes = [pltpu.make_async_copy(modes.at[k], held.at[k], in_sem.at[k]) for k in rows]
-    gives = [pltpu.make_async_copy(held.at[k], modes_out.at[k], out_sem.at[k]) for k in rows]
-    for take in takes:
-        take.start()
-    for take, give in zip(takes, gives):
-        take.wait()
-        give.start()
-    for give in gives:
-        give.wait()
+    give.wait()
 
 
 def per_device(table, energy_sum, snapshots, cell_weights, freq_order):
     n_tm = lax.axis_size("tm")
     cells = snapshots.shape[2]
     own = cells // n_tm
-    parts = 4
+    parts = 8
     width = own // parts
     scale = 1.0 / (energy_sum * COMP * cells * lax.axis_size("space"))
     factor = 1.0 / math.sqrt(energy_sum)
@@ -328,33 +336,33 @@
     weights = cell_weights.reshape(n_tm, own // 128, 128)
     dma = pltpu.SemaphoreType.DMA
     vmem = pl.BlockSpec(memory_space=pltpu.VMEM)
+    far = pl.BlockSpec(memory_space=pl.ANY)
     energies, modes = pl.pallas_call(
         functools.partial(kernel, parts, width, scale, factor),
         out_shape=(
-            jax.ShapeDtypeStruct((1, MODES), jnp.float32),
-            jax.ShapeDtypeStruct((MODES * COMP, 2, cells), jnp.bfloat16),
+            pltpu.VMEM((1, MODES), jnp.float32),
+            pltpu.VMEM((MODES * COMP, 2, cells), jnp.bfloat16),
         ),
-        in_specs=[
-            pl.BlockSpec(memory_space=pltpu.SMEM),
-            pl.BlockSpec(memory_space=pl.ANY),
-            pl.BlockSpec(memory_space=pl.ANY),
-            vmem,
-            vmem,
-        ],
-        out_specs=(vmem, pl.BlockSpec(memory_space=pl.ANY)),
+        in_specs=[far] * 5,
+        out_specs=(vmem, vmem),
         scratch_shapes=[
+            pltpu.SMEM((NF,), jnp.int32),
+            pltpu.VMEM((NF, 8, 128), jnp.float32),
+            pltpu.VMEM((2 * HALF, 128), jnp.float32),
+            pltpu.VMEM((own // 128, 128), jnp.float32),
             pltpu.VMEM((parts, COMP, n_tm * HALF, width), jnp.bfloat16),
-            pltpu.VMEM((own // 128, 128), jnp.float32),
             pltpu.VMEM((STRIP_ROWS, 2 * STRIP), jnp.bfloat16),
             pltpu.VMEM((STRIP_ROWS, STRIP), jnp.bfloat16),
-            pltpu.VMEM((COMP, STRIPS, STRIP_ROWS, width), jnp.float32),
-            pltpu.VMEM((GROUPS, parts, COMP, GROUP_ROWS, width), jnp.bfloat16),
+            pltpu.VMEM((STRIPS, STRIP_ROWS, COMP * width), jnp.float32),
+            pltpu.VMEM((GROUPS, parts, GROUP_ROWS, COMP * width), jnp.bfloat16),
             pltpu.VMEM((GROUPS, GROUP_ROWS, GROUP_ROWS), jnp.float32),
             pltpu.VMEM((NF, HALF // 2, 128), jnp.float32),
             pltpu.VMEM((n_tm, HALF // 2, 128), jnp.float32),
             pltpu.VMEM((lax.axis_size("space"), HALF // 2, 128), jnp.float32),
+            pltpu.VMEM((2 * MODES, 128), jnp.bfloat16),
             pltpu.VMEM((NF, 2 * MODES, 128), jnp.bfloat16),
             pltpu.VMEM((NF, MODES * COMP, 2, own), jnp.bfloat16),
+            dma((4,)),
             dma((parts,)),
             dma((parts,)),
             dma,
@@ -362,8 +370,7 @@
             dma,
             dma,
             dma,
-            dma,
-            dma,
+            dma((GROUPS,)),
             dma,
             dma,
         ],
@@ -378,15 +385,11 @@
             jax.ShapeDtypeStruct(energies.shape, energies.dtype),
             jax.ShapeDtypeStruct(modes.shape, modes.dtype),
         ),
-        in_specs=[vmem, pl.BlockSpec(memory_space=pl.ANY)],
-        out_specs=(vmem, pl.BlockSpec(memory_space=pl.ANY)),
-        scratch_shapes=[
-            pltpu.VMEM(modes.shape, modes.dtype),
-            dma((MODES * COMP,)),
-            dma((MODES * COMP,)),
-        ],
+        in_specs=[vmem, vmem],
+        out_specs=(vmem, far),
+        scratch_shapes=[dma],
         name="hand_over",
-    )(energies, modes)
+    )(*(pltpu.with_memory_space_constraint(x, pltpu.VMEM) for x in (energies, modes)))
     modes = modes.reshape(MODES, COMP, 2, cells).transpose(0, 2, 1, 3)
     return energies, modes[None]
 

time: 131 us -> 125 us (0.954)
  Pallas kernels: 130 us -> 125 us
    pallas_call x1, Pallas kernels: 126 us -> 123 us  [per_device(): pl.pallas_call(functools.partial(kernel, parts, width, scale, factor), ou...]
    pallas_call x1, Pallas kernels: 3.46 us -> 1.66 us  [per_device(): pl.pallas_call(hand_over, out_shape=(jax.ShapeDtypeStruct(energies.shape,...]
where the time goes in v3:
time: 125 us
  Pallas kernels  125 us (100%)
    pallas_call x1, Pallas kernels, per_device(): pl.pallas_call(functools.partial(kernel, parts, width, scale, factor), ou...  123 us

profile of v3, /device:TPU:1, one launch (start us, length us, event | category | flops | bytes accessed | tf_op | source)
XLA Modules:
  0.0 125.4 jit_solution(2652929566738385530)
XLA Ops:
  0.6 123.1 %spod.1 = (f32[1,4]{1,0:T(1,128)S(1)}, bf16[12,2,32768]{2,1,0:T(2,128)(2,1)S(1)}) custom-call(s32[32]{0:T(128)} %order_far.1, bf16[3,32,32768]{2,1,0:T(8,128)(2,1)} %bitcast.7, f32[32,8,128]{2,1,0:T(8,128)} %bitcast.8, f32[32,8,128]{2,1,0:T(8,128)} %constant.4.clone.table_far, f32[64,128]{1,0:T(8,128)} %constant.5.clone.start_far), custom_call_target="tpu_custom_call" | custom-call | tf_op jit(solution)/shard_map/spod/pallas_call | solution.py:340
  123.7 1.7 %hand_over.1 = (f32[1,4]{1,0:T(1,128)}, bf16[12,2,32768]{2,1,0:T(2,128)(2,1)}) custom-call(f32[1,4]{1,0:T(1,128)S(1)} %get-tuple-element.6.energies, bf16[12,2,32768]{2,1,0:T(2,128)(2,1)S(1)} %get-tuple-element.7.modes), custom_call_target="tpu_custom_call" | custom-call | tf_op jit(solution)/shard_map/hand_over/pallas_call | solution.py:382

commit v4 on v3

--- a/solution.py
+++ b/solution.py
@@ -30,7 +30,7 @@
 GROUPS = 8
 IN_GROUP = NF // GROUPS
 GROUP_ROWS = IN_GROUP * 2 * HALF
-GROUP_ORDER = (0, 1, 5, 2, 6, 4, 3, 7)
+GROUP_ORDER = (5, 2, 7, 4, 1, 6, 3, 0)
 STRIP = 8 * HALF
 STRIPS = 4
 STRIP_ROWS = 8 * 2 * NF
@@ -70,7 +70,11 @@
 
 
 def lane_halves_swapped(x, lane):
-    return jnp.where(lane < HALF, pltpu.roll(x, 128 - HALF, 1), pltpu.roll(x, HALF, 1))
+    return jnp.where(lane < HALF, shifted(x, -HALF), shifted(x, HALF))
+
+
+def shifted(x, lanes):
+    return pltpu.roll(x, lanes % 128, 1) if lanes % 128 else x
 
 
 def kernel(
@@ -178,24 +182,28 @@
             accumulate(part, g)
 
     lane = lax.broadcasted_iota(jnp.int32, (HALF, 128), 1)
-    low = lane < NFFT
-    half_low = low[: HALF // 2]
+    line = lax.broadcasted_iota(jnp.int32, (HALF, 128), 0)
+    quarter = lax.broadcasted_iota(jnp.int32, (8, 128), 1) // HALF
     transform(last_part)
 
     @pl.loop(0, GROUPS)
     def _(step):
-        g = lax.rem(home + step, GROUPS)
+        g = lax.rem(home + 5 * (step + 1), GROUPS)
         accumulate(last_part, g)
         for f in range(IN_GROUP):
             j = g * IN_GROUP + f
             tile = gram[g, f * NFFT : (f + 1) * NFFT, (f // 2) * 128 : (f // 2 + 1) * 128]
-            if f % 2:
-                tile = pltpu.roll(tile, NFFT, 1)
-            first, second = tile[:HALF], lane_halves_swapped(tile[HALF:], lane)
-            both = first + jnp.where(lane < HALF, second, -second)
-            gram_out[j] = jnp.where(
-                half_low, both[: HALF // 2], pltpu.roll(both[HALF // 2 :], NFFT, 1)
-            )
+            base = (f % 2) * NFFT
+            first, second = tile[:HALF], tile[HALF:]
+            real_part = first + shifted(second, -HALF)
+            imag_part = shifted(first, -HALF) - second
+            both = jnp.where(lane - base >= line, real_part, imag_part)
+            piece = both[:8]
+            piece = shifted(piece, -base)
+            for q in range(1, 4):
+                more = shifted(both[q * 8 : q * 8 + 8], q * HALF - base)
+                piece = jnp.where(quarter == q, more, piece)
+            gram_out[j] = piece
 
             @pl.when(j != me)
             def _():
@@ -222,10 +230,13 @@
         packed = packed + total[step]
     packed = packed * scale
 
-    near = jnp.concatenate([packed, pltpu.roll(packed, NFFT, 1)], axis=0)
-    near = jnp.where(low, near, 0.0)
-    top = jnp.where(lane < HALF, near, -near)
-    bottom = jnp.where(low, lane_halves_swapped(near, lane), 0.0)
+    both = jnp.concatenate([shifted(packed, -q * HALF) for q in range(4)], axis=0)
+    both = jnp.where(lane < HALF, both, 0.0)
+    across = jnp.concatenate([both, jnp.zeros((128 - HALF, 128), jnp.float32)], axis=0).T[:HALF]
+    real_part = jnp.where(lane >= line, both, across)
+    imag_part = jnp.where(lane < line, both, jnp.where(lane > line, -across, 0.0))
+    top = real_part - shifted(imag_part, HALF)
+    bottom = imag_part + shifted(real_part, HALF)
     matrix = jnp.concatenate([top, bottom], axis=0)
     empty = jnp.zeros((NFFT, 128), jnp.float32)
     column = lax.broadcasted_iota(jnp.int32, (NFFT, 128), 1)
@@ -240,12 +251,14 @@
     for _ in range(SWEEPS):
         vec = applied(vec)
         for k in range(MODES):
-            new = jnp.broadcast_to(vec[:, k : k + 1], (NFFT, 128))
-            new = new / jnp.sqrt(jnp.sum(new * new, axis=0, keepdims=True))
-            inner_re = jnp.sum(new * vec, axis=0, keepdims=True)
-            inner_im = jnp.sum(new * turned(vec), axis=0, keepdims=True)
-            less = vec - (inner_re * new - inner_im * turned(new))
-            vec = jnp.where(column == k, new, jnp.where(column > k, less, vec))
+            raw = jnp.broadcast_to(vec[:, k : k + 1], (NFFT, 128))
+            square = jnp.sum(raw * raw, axis=0, keepdims=True)
+            if k < MODES - 1:
+                inner_re = jnp.sum(raw * vec, axis=0, keepdims=True) / square
+                inner_im = jnp.sum(raw * turned(vec), axis=0, keepdims=True) / square
+                less = vec - (inner_re * raw - inner_im * turned(raw))
+                vec = jnp.where(column > k, less, vec)
+            vec = jnp.where(column == k, raw / jnp.sqrt(square), vec)
     vec = jnp.where(column < MODES, vec, 0.0)
 
     wide = lax.broadcasted_iota(jnp.int32, (8, 128), 1)
@@ -356,9 +369,9 @@
             pltpu.VMEM((STRIPS, STRIP_ROWS, COMP * width), jnp.float32),
             pltpu.VMEM((GROUPS, parts, GROUP_ROWS, COMP * width), jnp.bfloat16),
             pltpu.VMEM((GROUPS, GROUP_ROWS, GROUP_ROWS), jnp.float32),
-            pltpu.VMEM((NF, HALF // 2, 128), jnp.float32),
-            pltpu.VMEM((n_tm, HALF // 2, 128), jnp.float32),
-            pltpu.VMEM((lax.axis_size("space"), HALF // 2, 128), jnp.float32),
+            pltpu.VMEM((NF, 8, 128), jnp.float32),
+            pltpu.VMEM((n_tm, 8, 128), jnp.float32),
+            pltpu.VMEM((lax.axis_size("space"), 8, 128), jnp.float32),
             pltpu.VMEM((2 * MODES, 128), jnp.bfloat16),
             pltpu.VMEM((NF, 2 * MODES, 128), jnp.bfloat16),
             pltpu.VMEM((NF, MODES * COMP, 2, own), jnp.bfloat16),

time: 125 us -> 124 us (level)
  no operation moved by 1% of the time
where the time goes in v4:
time: 124 us
  Pallas kernels  124 us (100%)
    pallas_call x1, Pallas kernels, per_device(): pl.pallas_call(functools.partial(kernel, parts, width, scale, factor), ou...  122 us

profile of v4, /device:TPU:1, one launch (start us, length us, event | category | flops | bytes accessed | tf_op | source)
XLA Modules:
  0.0 124.4 jit_solution(10514957248587326031)
XLA Ops:
  0.6 122.1 %spod.1 = (f32[1,4]{1,0:T(1,128)S(1)}, bf16[12,2,32768]{2,1,0:T(2,128)(2,1)S(1)}) custom-call(s32[32]{0:T(128)} %order_far.1, bf16[3,32,32768]{2,1,0:T(8,128)(2,1)} %bitcast.7, f32[32,8,128]{2,1,0:T(8,128)} %bitcast.8, f32[32,8,128]{2,1,0:T(8,128)} %constant.4.clone.table_far, f32[64,128]{1,0:T(8,128)} %constant.5.clone.start_far), custom_call_target="tpu_custom_call" | custom-call | tf_op jit(solution)/shard_map/spod/pallas_call | solution.py:353
  122.7 1.7 %hand_over.1 = (f32[1,4]{1,0:T(1,128)}, bf16[12,2,32768]{2,1,0:T(2,128)(2,1)}) custom-call(f32[1,4]{1,0:T(1,128)S(1)} %get-tuple-element.6.energies, bf16[12,2,32768]{2,1,0:T(2,128)(2,1)S(1)} %get-tuple-element.7.modes), custom_call_target="tpu_custom_call" | custom-call | tf_op jit(solution)/shard_map/hand_over/pallas_call | solution.py:395

commit v5 on v4

--- a/solution.py
+++ b/solution.py
@@ -30,7 +30,6 @@
 GROUPS = 8
 IN_GROUP = NF // GROUPS
 GROUP_ROWS = IN_GROUP * 2 * HALF
-GROUP_ORDER = (5, 2, 7, 4, 1, 6, 3, 0)
 STRIP = 8 * HALF
 STRIPS = 4
 STRIP_ROWS = 8 * 2 * NF
@@ -279,9 +278,18 @@
     pltpu.make_async_copy(mine, mix.at[me], m_recv.at[home]).start()
     energies[...] = jnp.sum(vec * applied(vec), axis=0, keepdims=True)[:, :MODES]
 
+    sent = x_buf.at[:, :, pl.ds(0, (NF - 1) * HALF), :]
+    for part in range(parts):
+        pltpu.make_async_copy(sent.at[part], sent.at[part], x_send.at[part]).wait()
+    others = gram_out.at[pl.ds(0, NF - 1)]
+    pltpu.make_async_copy(others, others, g_send).wait()
+    others = total.at[pl.ds(0, n_space - 1)]
+    pltpu.make_async_copy(others, others, y_send).wait()
+
     span = pl.ds(pl.multiple_of(me * own, own), own)
-    for step in GROUP_ORDER:
-        g = lax.rem(home + step, GROUPS)
+    @pl.loop(0, GROUPS)
+    def _(step):
+        g = lax.rem(home + 5 * (step + 1), GROUPS)
         four = mix.at[pl.ds(g * IN_GROUP, IN_GROUP)]
         pltpu.make_async_copy(four, four, m_recv.at[g]).wait()
         zero = jnp.zeros((8, 128), jnp.float32)
@@ -316,13 +324,6 @@
             def _():
                 pltpu.make_async_copy(out_buf.at[j], modes.at[:, :, span], o_recv).start()
 
-    sent = x_buf.at[:, :, pl.ds(0, (NF - 1) * HALF), :]
-    for part in range(parts):
-        pltpu.make_async_copy(sent.at[part], sent.at[part], x_send.at[part]).wait()
-    others = gram_out.at[pl.ds(0, NF - 1)]
-    pltpu.make_async_copy(others, others, g_send).wait()
-    others = total.at[pl.ds(0, n_space - 1)]
-    pltpu.make_async_copy(others, others, y_send).wait()
     others = mix.at[pl.ds(0, NF - 1)]
     pltpu.make_async_copy(others, others, m_send).wait()
     others = out_buf.at[pl.ds(0, NF - 1)]
@@ -331,10 +332,15 @@
 
 
 def hand_over(energies, modes, energies_out, modes_out, sem):
-    give = pltpu.make_async_copy(modes, modes_out, sem)
-    give.start()
+    gives = [
+        pltpu.make_async_copy(modes.at[k], modes_out.at[k], sem.at[k])
+        for k in range(modes.shape[0])
+    ]
+    for give in gives:
+        give.start()
     energies_out[...] = energies[...]
-    give.wait()
+    for give in gives:
+        give.wait()
 
 
 def per_device(table, energy_sum, snapshots, cell_weights, freq_order):
@@ -400,7 +406,7 @@
         ),
         in_specs=[vmem, vmem],
         out_specs=(vmem, far),
-        scratch_shapes=[dma],
+        scratch_shapes=[dma((MODES * COMP,))],
         name="hand_over",
     )(*(pltpu.with_memory_space_constraint(x, pltpu.VMEM) for x in (energies, modes)))
     modes = modes.reshape(MODES, COMP, 2, cells).transpose(0, 2, 1, 3)

time: 124 us -> 125 us (level)
  no operation moved by 1% of the time
where the time goes in v5:
time: 125 us; the launch traced here: 124 us
  Pallas kernels  124 us (99%)
    pallas_call x1, Pallas kernels, per_device(): pl.pallas_call(functools.partial(kernel, parts, width, scale, factor), ou...  122 us

profile of v5, /device:TPU:1, one launch (start us, length us, event | category | flops | bytes accessed | tf_op | source)
XLA Modules:
  0.0 124.4 jit_solution(1151416986942797027)
XLA Ops:
  0.6 122.1 %spod.1 = (f32[1,4]{1,0:T(1,128)S(1)}, bf16[12,2,32768]{2,1,0:T(2,128)(2,1)S(1)}) custom-call(s32[32]{0:T(128)} %order_far.1, bf16[3,32,32768]{2,1,0:T(8,128)(2,1)} %bitcast.7, f32[32,8,128]{2,1,0:T(8,128)} %bitcast.8, f32[32,8,128]{2,1,0:T(8,128)} %constant.4.clone.table_far, f32[64,128]{1,0:T(8,128)} %constant.5.clone.start_far), custom_call_target="tpu_custom_call" | custom-call | tf_op jit(solution)/shard_map/spod/pallas_call | solution.py:359
  122.7 1.7 %hand_over.1 = (f32[1,4]{1,0:T(1,128)}, bf16[12,2,32768]{2,1,0:T(2,128)(2,1)}) custom-call(f32[1,4]{1,0:T(1,128)S(1)} %get-tuple-element.6.energies, bf16[12,2,32768]{2,1,0:T(2,128)(2,1)S(1)} %get-tuple-element.7.modes), custom_call_target="tpu_custom_call" | custom-call | tf_op jit(solution)/shard_map/hand_over/pallas_call | solution.py:401
